TPU v7x, 32 devices: a whole 2x2x4 slice. The times are simulated.
32 devices in a mesh: section: 2 (over core), expert: 4 (over z), tensor: 4 (over y, x).
Axes of the slice: x: 2, y: 2, z: 4, core: 2. Of those that a mesh axis runs over, the one named last changes fastest.
Arguments:
- tokens: bfloat16 [32, 197, 768], P('expert'), may hold values from -6 to 6
- batch_order: int32 [4, 8], P('expert'), may hold values from 0 to 7, each once within a row
- gain_attn: float32 [2, 768], P('section'), may hold values from 0.5 to 1.5
- shift_attn: float32 [2, 768], P('section'), may hold values from -3 to 3
- w_qkv: bfloat16 [2, 3, 768, 768], P('section', None, None, 'tensor'), may hold values from -0.21650635 to 0.21650635
- w_out: bfloat16 [2, 768, 768], P('section', 'tensor'), may hold values from -0.875 to 0.875
- gain_moe: float32 [2, 768], P('section'), may hold values from 0.5 to 1.5
- shift_moe: float32 [2, 768], P('section'), may hold values from -3 to 3
- w_router: float32 [2, 768, 8], P('section'), may hold values from -0.04330127 to 0.04330127
- w_in: bfloat16 [2, 8, 768, 3072], P('section', 'expert', None, 'tensor'), may hold values from -0.21875 to 0.21875
- w_back: bfloat16 [2, 8, 3072, 768], P('section', 'expert', 'tensor'), may hold values from -0.4375 to 0.4375
- routes: int32 [2, 32, 197, 2], P('section', 'expert'), may hold values from 0 to 7, as said below
- slots: int32 [2, 32, 197, 2], P('section', 'expert'), may hold values from -1 to 127, as said below
- cotangent: bfloat16 [32, 197, 768], P('expert'), may hold values from -6 to 6
Outputs:
- acts: bfloat16 [2, 32, 197, 768], P('section', 'expert')
- in_grads: float32 [2, 32, 197, 768], P('section', 'expert')
- grad_gain_attn: float32 [2, 768], P('section')
- grad_shift_attn: float32 [2, 768], P('section')
- grad_qkv: float32 [2, 3, 768, 768], P('section', None, None, 'tensor')
- grad_out: float32 [2, 768, 768], P('section', 'tensor')
- grad_gain_moe: float32 [2, 768], P('section')
- grad_shift_moe: float32 [2, 768], P('section')
- grad_router: float32 [2, 768, 8], P('section')
- grad_in: float32 [2, 8, 768, 3072], P('section', 'expert', None, 'tensor')
- grad_back: float32 [2, 8, 3072, 768], P('section', 'expert', 'tensor')
Inputs may be any that keep to these rules, and one draw needn't show every extreme that they name: `routes`: the two experts of a token differ. `slots`: within one layer and one block, choices are ranked first choices by row, then second choices by row, per expert; a choice's slot is its rank, -1 from rank 128 on.
All inputs are finite; a program needn't handle non-finite values.
Results may differ from a plain program's by a relative error of at most 0.019.
Values may be sent and summed in bfloat16 or wider, within the bound.
No kernel may reach another device: no remote copies, remote signals or barrier semaphores. Data moves between devices by JAX's collectives and lax.ppermute only.
A program may use at most 256 MiB of HBM per device.

v0:
```python
import jax
import jax.numpy as jnp
from jax import lax
from jax.sharding import PartitionSpec as P

HEAD = 64
TOPK = 2
SEQ = 197
MB = 4
IMG_MB = 2
NORM_EPS = 1e-06
HIGHEST = lax.Precision.HIGHEST


def from_behind(value, axis, steps):
    count = lax.axis_size(axis)
    first, last = (max(0, -steps), min(count, count - steps))
    return lax.ppermute(value, axis, [(source, source + steps) for source in range(first, last)])


def layer_norm(values, gain, shift):
    centred = values - jnp.mean(values, axis=-1, keepdims=True)
    inverse = lax.rsqrt(jnp.mean(centred * centred, axis=-1, keepdims=True) + NORM_EPS)
    unit_rows = centred * inverse
    return (unit_rows * gain + shift, unit_rows, inverse)


def norm_back(grad, unit_rows, inverse, gain):
    scaled = grad * gain
    inner = (
        scaled
        - jnp.mean(scaled, axis=-1, keepdims=True)
        - unit_rows * jnp.mean(scaled * unit_rows, axis=-1, keepdims=True)
    )
    return (inner * inverse, jnp.sum(grad * unit_rows, axis=0), jnp.sum(grad, axis=0))


def gelu_pair(pre_act):
    normal_cdf = 0.5 * (1.0 + jax.scipy.special.erf(pre_act * 0.7071067811865476))
    density = jnp.exp(-0.5 * pre_act * pre_act) * 0.3989422804014327
    return (pre_act * normal_cdf, normal_cdf + pre_act * density)


def slot_tables(route_block, slot_block, exp_dev, owners, capacity):
    owner_of = route_block // exp_dev
    local_of = route_block % exp_dev
    target = jnp.where(
        slot_block >= 0, local_of * (owners * capacity) + owner_of * capacity + slot_block, -1
    )
    columns = jnp.arange(exp_dev * owners * capacity, dtype=jnp.int32)
    return target[:, :, None] == columns[None, None, :]


def attention_forward(normed_low, wqkv, heads_local, block_rows):
    projected = jnp.einsum(
        "rd,idc->irc", normed_low, wqkv, preferred_element_type=jnp.float32
    ).astype(jnp.bfloat16)
    shaped = projected.reshape(3, IMG_MB, SEQ, heads_local, HEAD)
    scores = jnp.einsum(
        "ishd,ithd->ihst", shaped[0], shaped[1], preferred_element_type=jnp.float32
    ) * HEAD ** (-0.5)
    largest = jnp.max(scores, axis=-1, keepdims=True)
    shifted = jnp.exp(scores - largest)
    row_total = jnp.sum(shifted, axis=-1, keepdims=True)
    attn_probs = (shifted / row_total).astype(jnp.bfloat16)
    mixed_heads = jnp.einsum(
        "ihst,ithd->ishd", attn_probs, shaped[2], preferred_element_type=jnp.float32
    )
    return (
        projected,
        largest + jnp.log(row_total),
        mixed_heads.reshape(block_rows, -1).astype(jnp.bfloat16),
    )


def forward_layer(inputs, weights, route_block, slot_block, layout):
    gain_one, shift_one, wqkv, wout, gain_two, shift_two, wrouter, win, wback = weights
    exp_dev, owners, capacity, heads_local, model_width, block_rows = layout
    normed_a, unit_a, inverse_a = layer_norm(inputs, gain_one, shift_one)
    normed_low = normed_a.astype(jnp.bfloat16)
    projected, logsum, mixed_heads = attention_forward(normed_low, wqkv, heads_local, block_rows)
    attended = lax.psum(jnp.dot(mixed_heads, wout, preferred_element_type=jnp.float32), "tensor")
    hidden = inputs + attended
    normed_m, unit_m, inverse_m = layer_norm(hidden, gain_two, shift_two)
    router_probs = jax.nn.softmax(jnp.dot(normed_m, wrouter, precision=HIGHEST), axis=-1)
    choose = (
        route_block[:, :, None] == jnp.arange(wrouter.shape[1], dtype=jnp.int32)[None, None, :]
    ).astype(jnp.float32)
    gate_values = jnp.sum(router_probs[:, None, :] * choose, axis=-1)
    tables = slot_tables(route_block, slot_block, exp_dev, owners, capacity).astype(jnp.bfloat16)
    sent_rows = jnp.einsum(
        "rks,rd->sd", tables, normed_m.astype(jnp.bfloat16), preferred_element_type=jnp.float32
    ).astype(jnp.bfloat16)
    sent_rows = sent_rows.reshape(exp_dev, owners * capacity, model_width)
    arrived = lax.all_to_all(sent_rows, "expert", split_axis=1, concat_axis=1, tiled=True)
    pre_act = jnp.einsum("erd,edf->erf", arrived, win, preferred_element_type=jnp.float32)
    activated = gelu_pair(pre_act)[0].astype(jnp.bfloat16)
    partial_value = jnp.einsum("erf,efd->erd", activated, wback, preferred_element_type=jnp.float32)
    shares = lax.psum_scatter(partial_value, "tensor", scatter_dimension=2, tiled=True).astype(
        jnp.bfloat16
    )
    quarter = shares.shape[2]
    returned = lax.all_to_all(shares, "expert", split_axis=1, concat_axis=1, tiled=True).reshape(
        -1, quarter
    )
    selected_part = jnp.einsum("rks,sd->rkd", tables, returned, preferred_element_type=jnp.float32)
    hidden_part = lax.dynamic_slice_in_dim(hidden, lax.axis_index("tensor") * quarter, quarter, 1)
    output_part = hidden_part + jnp.sum(gate_values[:, :, None] * selected_part, axis=1)
    output, selected = (
        lax.all_gather(output_part, "tensor", axis=1, tiled=True),
        lax.all_gather(selected_part, "tensor", axis=2, tiled=True),
    )
    saved = (
        unit_a,
        inverse_a,
        normed_low,
        projected,
        logsum,
        mixed_heads,
        unit_m,
        inverse_m,
        normed_m,
        router_probs,
        choose,
        gate_values,
        tables,
        arrived,
        pre_act,
        selected,
    )
    return (output, saved)


def backward_layer(grad_output, weights, saved, layout):
    gain_one, shift_one, wqkv, wout, gain_two, shift_two, wrouter, win, wback = weights
    exp_dev, owners, capacity, heads_local, model_width, block_rows = layout
    (
        unit_a,
        inverse_a,
        normed_low,
        projected,
        logsum,
        mixed_heads,
        unit_m,
        inverse_m,
        normed_m,
        router_probs,
        choose,
        gate_values,
        tables,
        arrived,
        pre_act,
        selected,
    ) = saved
    grad_gates = jnp.sum(grad_output[:, None, :] * selected, axis=-1)
    activated, slope = gelu_pair(pre_act)
    quarter = model_width // lax.axis_size("tensor")
    grad_part = lax.dynamic_slice_in_dim(
        grad_output, lax.axis_index("tensor") * quarter, quarter, 1
    )
    weighted = (gate_values[:, :, None] * grad_part[:, None, :]).astype(jnp.bfloat16)
    grad_sent = jnp.einsum(
        "rks,rkd->sd", tables, weighted, preferred_element_type=jnp.float32
    ).astype(jnp.bfloat16)
    arrived_part = lax.all_to_all(
        grad_sent.reshape(exp_dev, owners * capacity, quarter),
        "expert",
        split_axis=1,
        concat_axis=1,
        tiled=True,
    )
    grad_arrived = lax.all_gather(arrived_part, "tensor", axis=2, tiled=True)
    grad_wback = jnp.einsum(
        "erf,erd->efd",
        activated.astype(jnp.bfloat16),
        grad_arrived,
        preferred_element_type=jnp.float32,
    )
    grad_pre = (
        jnp.einsum("erd,efd->erf", grad_arrived, wback, preferred_element_type=jnp.float32) * slope
    ).astype(jnp.bfloat16)
    grad_win = jnp.einsum("erd,erf->edf", arrived, grad_pre, preferred_element_type=jnp.float32)
    row_terms = jnp.einsum("erf,edf->erd", grad_pre, win, preferred_element_type=jnp.float32)
    grad_share = lax.psum_scatter(row_terms, "tensor", scatter_dimension=2, tiled=True).astype(
        jnp.bfloat16
    )
    home_part = lax.all_to_all(grad_share, "expert", split_axis=1, concat_axis=1, tiled=True)
    grad_home = lax.all_gather(home_part, "tensor", axis=2, tiled=True).reshape(-1, model_width)
    grad_norm_m = jnp.einsum("rks,sd->rd", tables, grad_home, preferred_element_type=jnp.float32)
    grad_probs = jnp.sum(choose * grad_gates[:, :, None], axis=1)
    grad_logits = router_probs * (
        grad_probs - jnp.sum(router_probs * grad_probs, axis=-1, keepdims=True)
    )
    grad_wrouter = jnp.einsum("rd,re->de", normed_m, grad_logits, precision=HIGHEST)
    grad_norm_m = grad_norm_m + jnp.einsum("re,de->rd", grad_logits, wrouter, precision=HIGHEST)
    grad_hidden_ln, grad_gain_two, grad_shift_two = norm_back(
        grad_norm_m, unit_m, inverse_m, gain_two
    )
    grad_hidden = grad_output + grad_hidden_ln
    grad_attn_low = grad_hidden.astype(jnp.bfloat16)
    grad_wout = jnp.einsum(
        "rc,rd->cd", mixed_heads, grad_attn_low, preferred_element_type=jnp.float32
    )
    grad_mixed = jnp.einsum(
        "rd,cd->rc", grad_attn_low, wout, preferred_element_type=jnp.float32
    ).astype(jnp.bfloat16)
    shaped = projected.reshape(3, IMG_MB, SEQ, heads_local, HEAD)
    score_scale = HEAD ** (-0.5)
    scores = (
        jnp.einsum("ishd,ithd->ihst", shaped[0], shaped[1], preferred_element_type=jnp.float32)
        * score_scale
    )
    attn_probs = jnp.exp(scores - logsum)
    grad_heads = grad_mixed.reshape(IMG_MB, SEQ, heads_local, HEAD)
    grad_values = jnp.einsum(
        "ihst,ishd->ithd",
        attn_probs.astype(jnp.bfloat16),
        grad_heads,
        preferred_element_type=jnp.float32,
    )
    grad_weights_soft = jnp.einsum(
        "ishd,ithd->ihst", grad_heads, shaped[2], preferred_element_type=jnp.float32
    )
    grad_scores = (
        attn_probs
        * (grad_weights_soft - jnp.sum(attn_probs * grad_weights_soft, axis=-1, keepdims=True))
    ).astype(jnp.bfloat16)
    grad_queries = (
        jnp.einsum("ihst,ithd->ishd", grad_scores, shaped[1], preferred_element_type=jnp.float32)
        * score_scale
    )
    grad_keys = (
        jnp.einsum("ihst,ishd->ithd", grad_scores, shaped[0], preferred_element_type=jnp.float32)
        * score_scale
    )
    grad_projected = (
        jnp.stack([grad_queries, grad_keys, grad_values])
        .reshape(3, block_rows, -1)
        .astype(jnp.bfloat16)
    )
    grad_wqkv = jnp.einsum(
        "rd,irc->idc", normed_low, grad_projected, preferred_element_type=jnp.float32
    )
    grad_normed_a = lax.psum(
        jnp.einsum("irc,idc->rd", grad_projected, wqkv, preferred_element_type=jnp.float32),
        "tensor",
    )
    grad_input_ln, grad_gain_one, grad_shift_one = norm_back(
        grad_normed_a, unit_a, inverse_a, gain_one
    )
    grad_input = grad_hidden + grad_input_ln
    return (
        grad_input,
        (
            grad_gain_one,
            grad_shift_one,
            grad_wqkv,
            grad_wout,
            grad_gain_two,
            grad_shift_two,
            grad_wrouter,
            grad_win,
            grad_wback,
        ),
    )


def shards(
    tokens,
    batch_order,
    gain_attn,
    shift_attn,
    w_qkv,
    w_out,
    gain_moe,
    shift_moe,
    w_router,
    w_in,
    w_back,
    routes,
    slots,
    cotangent,
):
    section_index = lax.axis_index("section")
    section_count = lax.axis_size("section")
    owners = lax.axis_size("expert")
    exp_dev = w_in.shape[1]
    experts = exp_dev * owners
    model_width = tokens.shape[2]
    block_rows = IMG_MB * SEQ
    capacity = (TOPK * block_rows * 5 // (4 * experts) + 7) // 8 * 8
    heads_local = w_qkv.shape[3] // HEAD
    layout = (exp_dev, owners, capacity, heads_local, model_width, block_rows)
    tick_count = MB + section_count - 1
    image_order = batch_order[0]
    weights = (
        gain_attn[0],
        shift_attn[0],
        w_qkv[0],
        w_out[0],
        gain_moe[0],
        shift_moe[0],
        w_router[0],
        w_in[0],
        w_back[0],
    )
    route_blocks = routes[0].reshape(MB, block_rows, TOPK)
    slot_blocks = slots[0].reshape(MB, block_rows, TOPK)
    inbound = jnp.zeros((block_rows, model_width), jnp.bfloat16)
    acts_store = jnp.zeros((MB, block_rows, model_width), jnp.bfloat16)
    kept_ticks = []
    for tick_index in range(tick_count):
        micro_index = tick_index - section_index
        active = (micro_index >= 0) & (micro_index < MB)
        clipped = jnp.clip(micro_index, 0, MB - 1)
        if tick_index < MB:
            fresh = jnp.take(
                tokens, image_order[tick_index * IMG_MB : (tick_index + 1) * IMG_MB], axis=0
            ).reshape(block_rows, model_width)
        else:
            fresh = jnp.zeros((block_rows, model_width), jnp.bfloat16)
        inputs = jnp.where(section_index == 0, fresh, inbound).astype(jnp.float32)
        route_block = lax.dynamic_index_in_dim(route_blocks, clipped, 0, keepdims=False)
        slot_block = lax.dynamic_index_in_dim(slot_blocks, clipped, 0, keepdims=False)
        output, saved = forward_layer(inputs, weights, route_block, slot_block, layout)
        output_low = output.astype(jnp.bfloat16)
        previous = lax.dynamic_index_in_dim(acts_store, clipped, 0, keepdims=False)
        acts_store = lax.dynamic_update_index_in_dim(
            acts_store, jnp.where(active, output_low, previous), clipped, 0
        )
        kept_ticks.append((saved, active, clipped))
        if tick_index + 1 < tick_count:
            inbound = from_behind(output_low, "section", 1)
    targets = jnp.take(cotangent, image_order, axis=0).reshape(MB, block_rows, model_width)
    grad_inbound = jnp.zeros((block_rows, model_width), jnp.bfloat16)
    grad_store = jnp.zeros((MB, block_rows, model_width), jnp.float32)
    totals = tuple((jnp.zeros(weight_item.shape, jnp.float32) for weight_item in weights))
    for back_index in range(tick_count):
        saved, active, clipped = kept_ticks[tick_count - 1 - back_index]
        target_rows = lax.dynamic_index_in_dim(targets, clipped, 0, keepdims=False)
        grad_output = jnp.where(
            section_index == section_count - 1, target_rows, grad_inbound
        ).astype(jnp.float32)
        grad_input, layer_grads = backward_layer(grad_output, weights, saved, layout)
        totals = tuple(
            (
                running + jnp.where(active, fresh_grad, 0.0)
                for running, fresh_grad in zip(totals, layer_grads)
            )
        )
        previous = lax.dynamic_index_in_dim(grad_store, clipped, 0, keepdims=False)
        grad_store = lax.dynamic_update_index_in_dim(
            grad_store, jnp.where(active, grad_input, previous), clipped, 0
        )
        if back_index + 1 < tick_count:
            grad_inbound = from_behind(grad_input.astype(jnp.bfloat16), "section", -1)
    shared = lax.psum(
        (totals[0], totals[1], totals[2], totals[3], totals[4], totals[5], totals[6]), "expert"
    )
    image_count = MB * IMG_MB
    acts_image = (
        jnp.zeros((image_count, SEQ, model_width), jnp.bfloat16)
        .at[image_order]
        .set(acts_store.reshape(image_count, SEQ, model_width))
    )
    grads_image = (
        jnp.zeros((image_count, SEQ, model_width), jnp.float32)
        .at[image_order]
        .set(grad_store.reshape(image_count, SEQ, model_width))
    )
    return (
        acts_image[None],
        grads_image[None],
        shared[0][None],
        shared[1][None],
        shared[2][None],
        shared[3][None],
        shared[4][None],
        shared[5][None],
        shared[6][None],
        totals[7][None],
        totals[8][None],
    )


def solution(mesh):
    return jax.shard_map(
        shards,
        mesh=mesh,
        in_specs=(
            P("expert", None, None),
            P("expert", None),
            P("section", None),
            P("section", None),
            P("section", None, None, "tensor"),
            P("section", "tensor", None),
            P("section", None),
            P("section", None),
            P("section", None, None),
            P("section", "expert", None, "tensor"),
            P("section", "expert", "tensor", None),
            P("section", "expert", None, None),
            P("section", "expert", None, None),
            P("expert", None, None),
        ),
        out_specs=(
            P("section", "expert", None, None),
            P("section", "expert", None, None),
            P("section", None),
            P("section", None),
            P("section", None, None, "tensor"),
            P("section", "tensor", None),
            P("section", None),
            P("section", None),
            P("section", None, None),
            P("section", "expert", None, "tensor"),
            P("section", "expert", "tensor", None),
        ),
        check_vma=False,
    )
```

profile of v0, /device:TPU:0, one launch (start us, length us, event | category | flops | bytes accessed | tf_op | source)
XLA Modules:
  0.0 2706.1 jit_solution(5228686551862741128)
XLA Ops:
  36.3 55.6 %all-reduce.14.cloned.1.call-done = f32[394,768]{0,1:T(8,128)} async-done(((f32[394,768]{0,1:T(8,128)}), f32[394,768]{0,1:T(8,128)}) %all-reduce.14.cloned.1.call-update) | async-done | bytes 1210384 | tf_op jit(solution)/shard_map/psum | solution.py:82
  98.9 41.3 %all_to_all.100 = bf16[2,512,768]{2,0,1:T(2,128)(2,1)} all-to-all(bf16[2,512,768]{2,0,1:T(2,128)(2,1)S(1)} %copy.1194), channel_id=1, replica_groups=mesh['section'=2,'expert'=4,'tensor'=4] {'expert'}, dimensions={1} | all-to-all | bytes 3145728 | tf_op jit(solution)/shard_map/all_to_all | solution.py:95
  153.5 42.1 %reduce-scatter.11.cloned.1.call-done = f32[2,512,192]{1,2,0:T(8,128)} async-done(((f32[2,512,768]{1,2,0:T(8,128)}), f32[2,512,192]{1,2,0:T(8,128)}) %reduce-scatter.11.cloned.1.call-update) | async-done | bytes 786448 | tf_op jit(solution)/shard_map/reduce_scatter | solution.py:99
  205.8 11.0 all-to-all-done.1
  223.4 11.7 all_gather.60
  272.3 57.2 %all-reduce.16.cloned.1.call-done = f32[394,768]{0,1:T(8,128)} async-done(((f32[394,768]{0,1:T(8,128)}), f32[394,768]{0,1:T(8,128)}) %all-reduce.16.cloned.1.call-update) | async-done | bytes 1210384 | tf_op jit(solution)/shard_map/psum | solution.py:82
  336.0 41.3 %all_to_all.101 = bf16[2,512,768]{2,0,1:T(2,128)(2,1)} all-to-all(bf16[2,512,768]{2,0,1:T(2,128)(2,1)S(1)} %copy.1211), channel_id=1, replica_groups=mesh['section'=2,'expert'=4,'tensor'=4] {'expert'}, dimensions={1} | all-to-all | bytes 3145728 | tf_op jit(solution)/shard_map/all_to_all | solution.py:95
  392.2 42.2 %reduce-scatter.13.cloned.1.call-done = f32[2,512,192]{1,2,0:T(8,128)} async-done(((f32[2,512,768]{1,2,0:T(8,128)}), f32[2,512,192]{1,2,0:T(8,128)}) %reduce-scatter.13.cloned.1.call-update) | async-done | bytes 786448 | tf_op jit(solution)/shard_map/reduce_scatter | solution.py:99
  444.0 11.6 all-to-all-done.3
  461.4 11.6 all_gather.61
  503.5 58.1 %all-reduce.18.cloned.1.call-done = f32[394,768]{0,1:T(8,128)} async-done(((f32[394,768]{0,1:T(8,128)}), f32[394,768]{0,1:T(8,128)}) %all-reduce.18.cloned.1.call-update) | async-done | bytes 1210384 | tf_op jit(solution)/shard_map/psum | solution.py:82
  568.0 41.3 %all_to_all.102 = bf16[2,512,768]{2,0,1:T(2,128)(2,1)} all-to-all(bf16[2,512,768]{2,0,1:T(2,128)(2,1)S(1)} %copy.1229), channel_id=1, replica_groups=mesh['section'=2,'expert'=4,'tensor'=4] {'expert'}, dimensions={1} | all-to-all | bytes 3145728 | tf_op jit(solution)/shard_map/all_to_all | solution.py:95
  624.3 42.2 %reduce-scatter.15.cloned.1.call-done = f32[2,512,192]{1,2,0:T(8,128)} async-done(((f32[2,512,768]{1,2,0:T(8,128)}), f32[2,512,192]{1,2,0:T(8,128)}) %reduce-scatter.15.cloned.1.call-update) | async-done | bytes 786448 | tf_op jit(solution)/shard_map/reduce_scatter | solution.py:99
  674.8 12.8 all-to-all-done.5
  690.6 11.8 all_gather.62
  715.2 58.7 %all-reduce.20.cloned.1.call-done = f32[394,768]{0,1:T(8,128)} async-done(((f32[394,768]{0,1:T(8,128)}), f32[394,768]{0,1:T(8,128)}) %all-reduce.20.cloned.1.call-update) | async-done | bytes 1210384 | tf_op jit(solution)/shard_map/psum | solution.py:82
  780.3 41.5 %all_to_all.103 = bf16[2,512,768]{2,0,1:T(2,128)(2,1)} all-to-all(bf16[2,512,768]{2,0,1:T(2,128)(2,1)S(1)} %copy.1247), channel_id=1, replica_groups=mesh['section'=2,'expert'=4,'tensor'=4] {'expert'}, dimensions={1} | all-to-all | bytes 3145728 | tf_op jit(solution)/shard_map/all_to_all | solution.py:95
  836.7 42.2 %reduce-scatter.17.cloned.1.call-done = f32[2,512,192]{1,2,0:T(8,128)} async-done(((f32[2,512,768]{1,2,0:T(8,128)}), f32[2,512,192]{1,2,0:T(8,128)}) %reduce-scatter.17.cloned.1.call-update) | async-done | bytes 786448 | tf_op jit(solution)/shard_map/reduce_scatter | solution.py:99
  887.1 13.0 all-to-all-done.7
  903.1 11.7 all_gather.63
  925.6 58.5 %all-reduce.22.cloned.1.call-done = f32[394,768]{0,1:T(8,128)} async-done(((f32[394,768]{0,1:T(8,128)}), f32[394,768]{0,1:T(8,128)}) %all-reduce.22.cloned.1.call-update) | async-done | bytes 1210384 | tf_op jit(solution)/shard_map/psum | solution.py:82
  989.2 41.3 %all_to_all.104 = bf16[2,512,768]{2,0,1:T(2,128)(2,1)} all-to-all(bf16[2,512,768]{2,0,1:T(2,128)(2,1)S(1)} %copy.1263), channel_id=1, replica_groups=mesh['section'=2,'expert'=4,'tensor'=4] {'expert'}, dimensions={1} | all-to-all | bytes 3145728 | tf_op jit(solution)/shard_map/all_to_all | solution.py:95
  1043.9 42.1 %reduce-scatter.19.cloned.1.call-done = f32[2,512,192]{1,2,0:T(8,128)} async-done(((f32[2,512,768]{1,2,0:T(8,128)}), f32[2,512,192]{1,2,0:T(8,128)}) %reduce-scatter.19.cloned.1.call-update) | async-done | bytes 786448 | tf_op jit(solution)/shard_map/reduce_scatter | solution.py:99
  1087.6 18.7 all_to_all.105
  1114.4 9.0 gather_fusion
  1143.6 9.7 all-gather.20.cloned.1.call-done
  1160.6 18.8 all_to_all.106
  1181.5 29.2 %all-gather.16.cloned.1.call-done = bf16[2,512,768]{1,2,0:T(8,128)(2,1)} async-done(((bf16[2,512,192]{1,2,0:T(8,128)(2,1)}), bf16[2,512,768]{1,2,0:T(8,128)(2,1)}) %all-gather.16.cloned.1.call-update) | async-done | bytes 1572880 | tf_op jit(solution)/shard_map/all_gather | solution.py:172
  1220.5 44.0 %reduce-scatter.21.cloned.1.call-done = f32[2,512,192]{1,2,0:T(8,128)} async-done(((f32[2,512,768]{1,2,0:T(8,128)}), f32[2,512,192]{1,2,0:T(8,128)}) %reduce-scatter.21.cloned.1.call-update) | async-done | bytes 786448 | tf_op jit(solution)/shard_map/reduce_scatter | solution.py:184
  1267.8 18.8 all_to_all.107
  1293.4 25.8 all-gather.18.cloned.1.call-done
  1338.4 60.8 %all-reduce.24.cloned.1.call-done = f32[394,768]{0,1:T(8,128)} async-done(((f32[394,768]{0,1:T(8,128)}), f32[394,768]{0,1:T(8,128)}) %all-reduce.24.cloned.1.call-update) | async-done | bytes 1210384 | tf_op jit(solution)/shard_map/psum | solution.py:244
  1415.3 19.3 all_to_all.108
  1436.8 28.9 %all-gather.22.cloned.1.call-done = bf16[2,512,768]{1,2,0:T(8,128)(2,1)} async-done(((bf16[2,512,192]{1,2,0:T(8,128)(2,1)}), bf16[2,512,768]{1,2,0:T(8,128)(2,1)}) %all-gather.22.cloned.1.call-update) | async-done | bytes 1572880 | tf_op jit(solution)/shard_map/all_gather | solution.py:172
  1476.1 43.4 %reduce-scatter.23.cloned.1.call-done = f32[2,512,192]{1,2,0:T(8,128)} async-done(((f32[2,512,768]{1,2,0:T(8,128)}), f32[2,512,192]{1,2,0:T(8,128)}) %reduce-scatter.23.cloned.1.call-update) | async-done | bytes 786448 | tf_op jit(solution)/shard_map/reduce_scatter | solution.py:184
  1522.8 18.8 all_to_all.109
  1545.2 19.9 all-gather.26.cloned.1.call-done
  1571.2 27.2 %all-gather.24.cloned.1.call-done = bf16[2,512,768]{1,0,2:T(2,128)(2,1)} async-done(((bf16[2,512,192]{1,0,2:T(2,128)(2,1)}), bf16[2,512,768]{1,0,2:T(2,128)(2,1)}) %all-gather.24.cloned.1.call-update) | async-done | bytes 1572880 | tf_op jit(solution)/shard_map/all_gather | solution.py:188
  1624.9 52.6 %all-reduce.26.cloned.1.call-done = f32[394,768]{0,1:T(8,128)} async-done(((f32[394,768]{0,1:T(8,128)}), f32[394,768]{0,1:T(8,128)}) %all-reduce.26.cloned.1.call-update) | async-done | bytes 1210384 | tf_op jit(solution)/shard_map/psum | solution.py:244
  1695.4 19.3 all_to_all.110
  1716.8 29.1 %all-gather.28.cloned.1.call-done = bf16[2,512,768]{1,2,0:T(8,128)(2,1)} async-done(((bf16[2,512,192]{1,2,0:T(8,128)(2,1)}), bf16[2,512,768]{1,2,0:T(8,128)(2,1)}) %all-gather.28.cloned.1.call-update) | async-done | bytes 1572880 | tf_op jit(solution)/shard_map/all_gather | solution.py:172
  1756.4 43.3 %reduce-scatter.25.cloned.1.call-done = f32[2,512,192]{1,2,0:T(8,128)} async-done(((f32[2,512,768]{1,2,0:T(8,128)}), f32[2,512,192]{1,2,0:T(8,128)}) %reduce-scatter.25.cloned.1.call-update) | async-done | bytes 786448 | tf_op jit(solution)/shard_map/reduce_scatter | solution.py:184
  1803.0 18.8 all_to_all.111
  1825.8 19.6 all-gather.32.cloned.1.call-done
  1851.6 27.0 all-gather.30.cloned.1.call-done
  1905.2 52.5 %all-reduce.28.cloned.1.call-done = f32[394,768]{0,1:T(8,128)} async-done(((f32[394,768]{0,1:T(8,128)}), f32[394,768]{0,1:T(8,128)}) %all-reduce.28.cloned.1.call-update) | async-done | bytes 1210384 | tf_op jit(solution)/shard_map/psum | solution.py:244
  1975.6 19.3 all_to_all.112
  1997.1 28.9 %all-gather.34.cloned.1.call-done = bf16[2,512,768]{1,2,0:T(8,128)(2,1)} async-done(((bf16[2,512,192]{1,2,0:T(8,128)(2,1)}), bf16[2,512,768]{1,2,0:T(8,128)(2,1)}) %all-gather.34.cloned.1.call-update) | async-done | bytes 1572880 | tf_op jit(solution)/shard_map/all_gather | solution.py:172
  2036.5 43.3 %reduce-scatter.27.cloned.1.call-done = f32[2,512,192]{1,2,0:T(8,128)} async-done(((f32[2,512,768]{1,2,0:T(8,128)}), f32[2,512,192]{1,2,0:T(8,128)}) %reduce-scatter.27.cloned.1.call-update) | async-done | bytes 786448 | tf_op jit(solution)/shard_map/reduce_scatter | solution.py:184
  2083.1 18.8 all_to_all.113
  2105.5 20.0 all-gather.38.cloned.1.call-done
  2131.6 27.2 %all-gather.36.cloned.1.call-done = bf16[2,512,768]{1,0,2:T(2,128)(2,1)} async-done(((bf16[2,512,192]{1,0,2:T(2,128)(2,1)}), bf16[2,512,768]{1,0,2:T(2,128)(2,1)}) %all-gather.36.cloned.1.call-update) | async-done | bytes 1572880 | tf_op jit(solution)/shard_map/all_gather | solution.py:188
  2198.3 49.9 %all-reduce.30.cloned.1.call-done = f32[394,768]{0,1:T(8,128)} async-done(((f32[394,768]{0,1:T(8,128)}), f32[394,768]{0,1:T(8,128)}) %all-reduce.30.cloned.1.call-update) | async-done | bytes 1210384 | tf_op jit(solution)/shard_map/psum | solution.py:244
  2273.5 19.3 all_to_all.114
  2294.8 29.1 %all-gather.40.cloned.1.call-done = bf16[2,512,768]{1,2,0:T(8,128)(2,1)} async-done(((bf16[2,512,192]{1,2,0:T(8,128)(2,1)}), bf16[2,512,768]{1,2,0:T(8,128)(2,1)}) %all-gather.40.cloned.1.call-update) | async-done | bytes 1572880 | tf_op jit(solution)/shard_map/all_gather | solution.py:172
  2381.5 16.4 all_gather.64
  2408.7 6.5 scatter_fusion
  2492.4 7.9 add_bitcast_fusion
  2500.3 13.2 all-gather.42.cloned.1.call-done
  2544.6 10.2 add_bitcast_fusion.1
  2554.9 41.4 %all-reduce.32.cloned.1.call-done = f32[394,768]{0,1:T(8,128)} async-done(((f32[394,768]{0,1:T(8,128)}), f32[394,768]{0,1:T(8,128)}) %all-reduce.32.cloned.1.call-update) | async-done | bytes 1210384 | tf_op jit(solution)/shard_map/psum | solution.py:244
  2612.6 8.7 scatter_fusion.1
  2627.8 21.7 all-reduce
  2649.5 45.8 %all-reduce.34.cloned.1.call-done = (f32[1,3,768,192]{2,3,1,0:T(8,128)}, f32[1,192,768]{2,1,0:T(8,128)}) async-done(((f32[1,3,768,192]{2,3,1,0:T(8,128)}, f32[1,192,768]{2,1,0:T(8,128)}), (f32[1,3,768,192]{2,3,1,0:T(8,128)}, f32[1,192,768]{2,1,0:T(8,128)})) %all-reduce.34.cloned.1.call-update) | async-done | bytes 2359312 | tf_op jit(solution)/shard_map/psum | solution.py:357
  (1402 shorter events, 803.1 us)
Async XLA Ops:
  7.2 84.7 %all-reduce.14.cloned.1.call-start = ((), (), s32[]{:S(2)}) async-start(), calls=%async_computation.30 | async-start | bytes 3145728 | tf_op jit(solution)/shard_map/psum | solution.py:82
  9.4 487.3 %copy-start.229 = (f32[768]{0:T(1024)}, f32[768]{0:T(1024)S(1)}, u32[]{:S(2)}) copy-start(f32[768]{0:T(1024)S(1)} %reduce.3) | copy-start | bytes 9220
  28.2 167.4 %reduce-scatter.11.cloned.1.call-start = ((), (), s32[]{:S(2)}) async-start(), calls=%async_computation.31 | async-start | bytes 3932160 | tf_op jit(solution)/shard_map/reduce_scatter | solution.py:99
  35.0 184.8 %copy-start.319 = (s32[394,2]{0,1:T(2,128)}, s32[394,2]{0,1:T(2,128)S(1)}, u32[]{:S(2)}) copy-start(s32[394,2]{0,1:T(2,128)S(1)} %compare_select_fusion.4) | copy-start | bytes 9460
  197.9 18.9 all-to-all-start.1
  202.5 127.0 %all-reduce.16.cloned.1.call-start = ((), (), s32[]{:S(2)}) async-start(), calls=%async_computation.32 | async-start | bytes 3145728 | tf_op jit(solution)/shard_map/psum | solution.py:82
  236.1 15.3 collective-permute-start
  270.1 164.3 %reduce-scatter.13.cloned.1.call-start = ((), (), s32[]{:S(2)}) async-start(), calls=%async_computation.33 | async-start | bytes 3932160 | tf_op jit(solution)/shard_map/reduce_scatter | solution.py:99
  271.0 187.6 %copy-start.321 = (s32[394,2]{0,1:T(2,128)}, s32[394,2]{0,1:T(2,128)S(1)}, u32[]{:S(2)}) copy-start(s32[394,2]{0,1:T(2,128)S(1)} %compare_select_fusion.3) | copy-start | bytes 9460
  331.3 109.9 %copy-start.218 = (f32[394]{0:T(512)}, f32[394]{0:T(512)S(1)}, u32[]{:S(2)}) copy-start(f32[394]{0:T(512)S(1)} %broadcast_multiply_fusion.27) | copy-start | bytes 4732
  436.6 18.9 all-to-all-start.3
  441.2 120.3 %all-reduce.18.cloned.1.call-start = ((), (), s32[]{:S(2)}) async-start(), calls=%async_computation.34 | async-start | bytes 3145728 | tf_op jit(solution)/shard_map/psum | solution.py:82
  474.2 19.7 collective-permute-start.1
  502.1 164.3 %reduce-scatter.15.cloned.1.call-start = ((), (), s32[]{:S(2)}) async-start(), calls=%async_computation.35 | async-start | bytes 3932160 | tf_op jit(solution)/shard_map/reduce_scatter | solution.py:99
  502.2 186.5 %copy-start.323 = (s32[394,2]{0,1:T(2,128)}, s32[394,2]{0,1:T(2,128)S(1)}, u32[]{:S(2)}) copy-start(s32[394,2]{0,1:T(2,128)S(1)} %compare_select_fusion.2) | copy-start | bytes 9460
  563.3 127.2 %copy-start.8 = (f32[394,768]{0,1:T(8,128)}, f32[394,768]{0,1:T(8,128)S(1)}, u32[]{:S(2)}) copy-start(f32[394,768]{0,1:T(8,128)S(1)} %get-tuple-element.147) | copy-start | bytes 3631108
  563.3 110.2 %copy-start.220 = (f32[394]{0:T(512)}, f32[394]{0:T(512)S(1)}, u32[]{:S(2)}) copy-start(f32[394]{0:T(512)S(1)} %broadcast_multiply_fusion.25) | copy-start | bytes 4732
  668.7 18.9 all-to-all-start.5
  673.3 100.6 %all-reduce.20.cloned.1.call-start = ((), (), s32[]{:S(2)}) async-start(), calls=%async_computation.36 | async-start | bytes 3145728 | tf_op jit(solution)/shard_map/psum | solution.py:82
  703.5 3.2 collective-permute-start.2
  713.9 165.0 %reduce-scatter.17.cloned.1.call-start = ((), (), s32[]{:S(2)}) async-start(), calls=%async_computation.37 | async-start | bytes 3932160 | tf_op jit(solution)/shard_map/reduce_scatter | solution.py:99
  714.0 187.3 %copy-start.325 = (s32[394,2]{0,1:T(2,128)}, s32[394,2]{0,1:T(2,128)S(1)}, u32[]{:S(2)}) copy-start(s32[394,2]{0,1:T(2,128)S(1)} %compare_select_fusion.1) | copy-start | bytes 9460
  775.6 127.4 %copy-start.11 = (f32[394,768]{0,1:T(8,128)}, f32[394,768]{0,1:T(8,128)S(1)}, u32[]{:S(2)}) copy-start(f32[394,768]{0,1:T(8,128)S(1)} %get-tuple-element.141) | copy-start | bytes 3631108
  775.6 110.1 %copy-start.223 = (f32[394]{0:T(512)}, f32[394]{0:T(512)S(1)}, u32[]{:S(2)}) copy-start(f32[394]{0:T(512)S(1)} %broadcast_multiply_fusion.23) | copy-start | bytes 4732
  881.2 18.9 all-to-all-start.7
  885.8 98.4 %all-reduce.22.cloned.1.call-start = ((), (), s32[]{:S(2)}) async-start(), calls=%async_computation.38 | async-start | bytes 3145728 | tf_op jit(solution)/shard_map/psum | solution.py:82
  916.0 3.1 collective-permute-start.3
  924.7 161.3 %reduce-scatter.19.cloned.1.call-start = ((), (), s32[]{:S(2)}) async-start(), calls=%async_computation.39 | async-start | bytes 3932160 | tf_op jit(solution)/shard_map/reduce_scatter | solution.py:99
  1043.8 109.5 %all-gather.20.cloned.1.call-start = ((), (), s32[]{:S(2)}) async-start(), calls=%async_computation.43 | async-start | bytes 3932160 | tf_op jit(solution)/shard_map/all_gather | solution.py:111
  1111.2 99.5 %all-gather.16.cloned.1.call-start = ((), (), s32[]{:S(2)}) async-start(), calls=%async_computation.40 | async-start | bytes 1966080 | tf_op jit(solution)/shard_map/all_gather | solution.py:172
  1143.6 146.7 %copy-start.188 = (f32[394,8]{0,1:T(8,128)}, f32[394,8]{0,1:T(8,128)S(1)}, u32[]{:S(2)}) copy-start(f32[394,8]{0,1:T(8,128)S(1)} %fusion.421) | copy-start | bytes 37828
  1156.3 134.0 %copy-start.190 = (f32[394,8]{0,1:T(8,128)}, f32[394,8]{0,1:T(8,128)S(1)}, u32[]{:S(2)}) copy-start(f32[394,8]{0,1:T(8,128)S(1)} %get-tuple-element.129) | copy-start | bytes 37828
  1181.4 83.1 %reduce-scatter.21.cloned.1.call-start = ((), (), s32[]{:S(2)}) async-start(), calls=%async_computation.41 | async-start | bytes 3932160 | tf_op jit(solution)/shard_map/reduce_scatter | solution.py:184
  1220.4 98.8 %all-gather.18.cloned.1.call-start = ((), (), s32[]{:S(2)}) async-start(), calls=%async_computation.42 | async-start | bytes 1966080 | tf_op jit(solution)/shard_map/all_gather | solution.py:188
  1290.1 109.1 %all-reduce.24.cloned.1.call-start = ((), (), s32[]{:S(2)}) async-start(), calls=%async_computation.44 | async-start | bytes 3145728 | tf_op jit(solution)/shard_map/psum | solution.py:244
  1338.3 127.4 %all-gather.22.cloned.1.call-start = ((), (), s32[]{:S(2)}) async-start(), calls=%async_computation.45 | async-start | bytes 1966080 | tf_op jit(solution)/shard_map/all_gather | solution.py:172
  1405.4 3.9 collective-permute-start.4
  1410.9 154.2 %copy-start.65 = (f32[394,768]{0,1:T(8,128)}, f32[394,768]{0,1:T(8,128)S(1)}, u32[]{:S(2)}) copy-start(f32[394,768]{0,1:T(8,128)S(1)} %fusion.268) | copy-start | bytes 3631108
  1436.6 83.0 %reduce-scatter.23.cloned.1.call-start = ((), (), s32[]{:S(2)}) async-start(), calls=%async_computation.46 | async-start | bytes 3932160 | tf_op jit(solution)/shard_map/reduce_scatter | solution.py:184
  1475.5 89.6 %all-gather.26.cloned.1.call-start = ((), (), s32[]{:S(2)}) async-start(), calls=%async_computation.48 | async-start | bytes 3932160 | tf_op jit(solution)/shard_map/all_gather | solution.py:111
  1476.1 122.3 %all-gather.24.cloned.1.call-start = ((), (), s32[]{:S(2)}) async-start(), calls=%async_computation.47 | async-start | bytes 1966080 | tf_op jit(solution)/shard_map/all_gather | solution.py:188
  1545.1 132.5 %all-reduce.26.cloned.1.call-start = ((), (), s32[]{:S(2)}) async-start(), calls=%async_computation.49 | async-start | bytes 3145728 | tf_op jit(solution)/shard_map/psum | solution.py:244
  1616.7 129.2 %all-gather.28.cloned.1.call-start = ((), (), s32[]{:S(2)}) async-start(), calls=%async_computation.50 | async-start | bytes 1966080 | tf_op jit(solution)/shard_map/all_gather | solution.py:172
  1685.6 3.9 collective-permute-start.5
  1691.0 154.4 %copy-start.67 = (f32[394,768]{0,1:T(8,128)}, f32[394,768]{0,1:T(8,128)S(1)}, u32[]{:S(2)}) copy-start(f32[394,768]{0,1:T(8,128)S(1)} %fusion.267) | copy-start | bytes 3631108
  1716.7 83.0 %reduce-scatter.25.cloned.1.call-start = ((), (), s32[]{:S(2)}) async-start(), calls=%async_computation.51 | async-start | bytes 3932160 | tf_op jit(solution)/shard_map/reduce_scatter | solution.py:184
  1755.7 89.8 %all-gather.32.cloned.1.call-start = ((), (), s32[]{:S(2)}) async-start(), calls=%async_computation.53 | async-start | bytes 3932160 | tf_op jit(solution)/shard_map/all_gather | solution.py:111
  1756.4 122.2 %all-gather.30.cloned.1.call-start = ((), (), s32[]{:S(2)}) async-start(), calls=%async_computation.52 | async-start | bytes 1966080 | tf_op jit(solution)/shard_map/all_gather | solution.py:188
  1825.3 132.4 %all-reduce.28.cloned.1.call-start = ((), (), s32[]{:S(2)}) async-start(), calls=%async_computation.54 | async-start | bytes 3145728 | tf_op jit(solution)/shard_map/psum | solution.py:244
  1896.8 129.2 %all-gather.34.cloned.1.call-start = ((), (), s32[]{:S(2)}) async-start(), calls=%async_computation.55 | async-start | bytes 1966080 | tf_op jit(solution)/shard_map/all_gather | solution.py:172
  1965.7 3.9 collective-permute-start.6
  1971.2 154.4 %copy-start.69 = (f32[394,768]{0,1:T(8,128)}, f32[394,768]{0,1:T(8,128)S(1)}, u32[]{:S(2)}) copy-start(f32[394,768]{0,1:T(8,128)S(1)} %fusion.266) | copy-start | bytes 3631108
  1996.9 82.9 %reduce-scatter.27.cloned.1.call-start = ((), (), s32[]{:S(2)}) async-start(), calls=%async_computation.56 | async-start | bytes 3932160 | tf_op jit(solution)/shard_map/reduce_scatter | solution.py:184
  2035.7 89.8 %all-gather.38.cloned.1.call-start = ((), (), s32[]{:S(2)}) async-start(), calls=%async_computation.58 | async-start | bytes 3932160 | tf_op jit(solution)/shard_map/all_gather | solution.py:111
  2036.5 122.3 %all-gather.36.cloned.1.call-start = ((), (), s32[]{:S(2)}) async-start(), calls=%async_computation.57 | async-start | bytes 1966080 | tf_op jit(solution)/shard_map/all_gather | solution.py:188
  2105.4 142.8 %all-reduce.30.cloned.1.call-start = ((), (), s32[]{:S(2)}) async-start(), calls=%async_computation.59 | async-start | bytes 3145728 | tf_op jit(solution)/shard_map/psum | solution.py:244
  2187.3 136.5 %all-gather.40.cloned.1.call-start = ((), (), s32[]{:S(2)}) async-start(), calls=%async_computation.60 | async-start | bytes 1966080 | tf_op jit(solution)/shard_map/all_gather | solution.py:172
  2257.1 4.3 collective-permute-start.7
  2294.7 165.7 %reduce-scatter.29.cloned.1.call-start = ((), (), s32[]{:S(2)}) async-start(), calls=%async_computation.61 | async-start | bytes 3932160 | tf_op jit(solution)/shard_map/reduce_scatter | solution.py:184
  2333.7 148.8 %all-gather.44.cloned.1.call-start = ((), (), s32[]{:S(2)}) async-start(), calls=%async_computation.63 | async-start | bytes 3932160 | tf_op jit(solution)/shard_map/all_gather | solution.py:111
  2462.7 17.7 all-to-all-start.19
  2467.3 46.3 %all-gather.42.cloned.1.call-start = ((), (), s32[]{:S(2)}) async-start(), calls=%async_computation.62 | async-start | bytes 1966080 | tf_op jit(solution)/shard_map/all_gather | solution.py:188
  2482.2 114.1 %all-reduce.32.cloned.1.call-start = ((), (), s32[]{:S(2)}) async-start(), calls=%async_computation.64 | async-start | bytes 3145728 | tf_op jit(solution)/shard_map/psum | solution.py:244
  2535.4 159.9 %all-reduce.34.cloned.1.call-start = ((), (), s32[]{:S(2)}) async-start(), calls=%async_computation.65 | async-start | bytes 4718592 | tf_op jit(solution)/shard_map/psum | solution.py:357
  (366 other events, 3989.5 us)
Sparse Core Ops, SparseCore 0:
  28.3 63.4 all-reduce.13
  153.5 42.0 reduce-scatter.10
  270.2 59.2 all-reduce.15
  392.3 42.0 reduce-scatter.12
  502.2 59.2 all-reduce.17
  624.4 42.0 reduce-scatter.14
  714.0 59.8 all-reduce.19
  836.8 42.0 reduce-scatter.16
  924.8 59.2 all-reduce.21
  1044.0 42.0 reduce-scatter.18
  1111.3 41.9 all-gather.19
  1181.6 29.0 all-gather.15
  1220.6 43.8 reduce-scatter.20
  1290.2 28.9 all-gather.17
  1338.4 60.7 all-reduce.23
  1436.7 28.9 all-gather.21
  1475.6 43.8 reduce-scatter.22
  1521.2 43.8 all-gather.25
  1567.5 30.8 all-gather.23
  1616.8 60.7 all-reduce.25
  1716.8 28.9 all-gather.27
  1755.8 43.8 reduce-scatter.24
  1801.6 43.8 all-gather.31
  1847.7 30.8 all-gather.29
  1896.9 60.7 all-reduce.27
  1997.0 28.9 all-gather.33
  2035.9 43.8 reduce-scatter.26
  2081.6 43.8 all-gather.37
  2127.9 30.8 all-gather.35
  2187.4 60.7 all-reduce.29
  2294.8 28.9 all-gather.39
  2333.8 43.8 reduce-scatter.28
  2379.4 45.9 all-gather.43
  2482.2 31.2 all-gather.41
  2535.5 60.7 all-reduce.31
  2599.1 96.1 all-reduce.33
where the time goes:
time: 2720 us; the launch traced here: 2710 us
  waiting for transfers between devices  1370 us (50%)
  blocking collectives  482 us (18%)
  local copies, waits for them, and re-layouts  397 us (15%)
  matrix products  269 us (10%)
  other arithmetic  125 us (5%)
  starting transfers between devices  39.8 us (1%)
    psum x5, waiting for transfers between devices, forward_layer(): lax.psum(jnp.dot(mixed_heads, wout, preferred_element_type=jnp.float32),...  288 us
    psum x5, waiting for transfers between devices, backward_layer(): lax.psum(jnp.einsum('irc,idc->rd', grad_projected, wqkv, preferred_elemen...  257 us
    reduce_scatter x5, waiting for transfers between devices, forward_layer(): lax.psum_scatter(partial_value, 'tensor', scatter_dimension=2, tiled=True)  211 us
    all_to_all x5, blocking collectives, forward_layer(): lax.all_to_all(sent_rows, 'expert', split_axis=1, concat_axis=1, tiled=True)  207 us
    reduce_scatter x5, waiting for transfers between devices, backward_layer(): lax.psum_scatter(row_terms, 'tensor', scatter_dimension=2, tiled=True)  174 us
    all_gather x5, waiting for transfers between devices, backward_layer(): grad_arrived = lax.all_gather(arrived_part, 'tensor', axis=2, tiled=True)  145 us
    all_gather x5, waiting for transfers between devices, backward_layer(): lax.all_gather(home_part, 'tensor', axis=2, tiled=True)  120 us
    all_to_all x5, blocking collectives, backward_layer(): lax.all_to_all(grad_sent.reshape(exp_dev, owners * capacity, quarter), 'e...  96 us
  transfers between devices with their start and end apart: 49, of which 43 were waited for; matrix products, arithmetic and copies ran while one was open for 12% of the time, Pallas kernels for 0%

commit v1 on v0

--- a/solution.py
+++ b/solution.py
@@ -1,3 +1,4 @@
+import functools
 import jax
 import jax.numpy as jnp
 from jax import lax
@@ -10,6 +11,15 @@
 IMG_MB = 2
 NORM_EPS = 1e-06
 HIGHEST = lax.Precision.HIGHEST
+
+
+def _set_state(panel, axis_id):
+    f_now = lax.all_gather(panel, axis_id)
+    all_values = jnp.sum(f_now, axis=0)
+    return all_values
+
+
+note_the_sector = functools.partial(_set_state, axis_id="tensor")
 
 
 def from_behind(value, axis, steps):
@@ -79,7 +89,7 @@
     normed_a, unit_a, inverse_a = layer_norm(inputs, gain_one, shift_one)
     normed_low = normed_a.astype(jnp.bfloat16)
     projected, logsum, mixed_heads = attention_forward(normed_low, wqkv, heads_local, block_rows)
-    attended = lax.psum(jnp.dot(mixed_heads, wout, preferred_element_type=jnp.float32), "tensor")
+    attended = note_the_sector(jnp.dot(mixed_heads, wout, preferred_element_type=jnp.float32))
     hidden = inputs + attended
     normed_m, unit_m, inverse_m = layer_norm(hidden, gain_two, shift_two)
     router_probs = jax.nn.softmax(jnp.dot(normed_m, wrouter, precision=HIGHEST), axis=-1)

time: 2720 us -> 2720 us (level)
    psum x5 -> x0, waiting for transfers between devices: 288 us -> none  [forward_layer(): lax.psum(jnp.dot(mixed_heads, wout, preferred_element_type=jnp.float32),...]
    all_gather x0 -> x5, waiting for transfers between devices: none -> 275 us  [_set_state(): f_now = lax.all_gather(panel, axis_id)]
    unnamed x786 -> x780, local copies, waits for them, and re-layouts: 74.9 us -> 67.8 us
where the time goes in v1:
time: 2720 us; the launch traced here: 2710 us
  waiting for transfers between devices  1370 us (50%)
  blocking collectives  481 us (18%)
  local copies, waits for them, and re-layouts  385 us (14%)
  matrix products  265 us (10%)
  other arithmetic  148 us (5%)
  starting transfers between devices  39.8 us (1%)
    all_gather x5, waiting for transfers between devices, _set_state(): f_now = lax.all_gather(panel, axis_id)  275 us
    psum x5, waiting for transfers between devices, backward_layer(): lax.psum(jnp.einsum('irc,idc->rd', grad_projected, wqkv, preferred_elemen...  257 us
    all_to_all x5, blocking collectives, forward_layer(): lax.all_to_all(sent_rows, 'expert', split_axis=1, concat_axis=1, tiled=True)  207 us
    reduce_scatter x5, waiting for transfers between devices, forward_layer(): lax.psum_scatter(partial_value, 'tensor', scatter_dimension=2, tiled=True)  203 us
    reduce_scatter x5, waiting for transfers between devices, backward_layer(): lax.psum_scatter(row_terms, 'tensor', scatter_dimension=2, tiled=True)  174 us
    all_gather x5, waiting for transfers between devices, backward_layer(): grad_arrived = lax.all_gather(arrived_part, 'tensor', axis=2, tiled=True)  145 us
    all_gather x5, waiting for transfers between devices, backward_layer(): lax.all_gather(home_part, 'tensor', axis=2, tiled=True)  123 us
    all_to_all x5, blocking collectives, backward_layer(): lax.all_to_all(grad_sent.reshape(exp_dev, owners * capacity, quarter), 'e...  95.4 us
  transfers between devices with their start and end apart: 49, of which 43 were waited for; matrix products, arithmetic and copies ran while one was open for 12% of the time, Pallas kernels for 0%

profile of v1, /device:TPU:0, one launch (start us, length us, event | category | flops | bytes accessed | tf_op | source)
XLA Modules:
  0.0 2708.0 jit_solution(5512992514575595094)
XLA Ops:
  44.8 51.9 %all-gather.61.cloned.1.call-done = f32[4,394,768]{2,1,0:T(8,128)} async-done(((f32[1,394,768]{2,1,0:T(8,128)}), f32[4,394,768]{2,1,0:T(8,128)}) %all-gather.61.cloned.1.call-update) | async-done | bytes 4841488 | tf_op jit(solution)/shard_map/all_gather | solution.py:17
  117.9 41.5 %all_to_all.100 = bf16[2,512,768]{2,0,1:T(2,128)(2,1)} all-to-all(bf16[2,512,768]{2,0,1:T(2,128)(2,1)S(1)} %copy.1223), channel_id=1, replica_groups=mesh['section'=2,'expert'=4,'tensor'=4] {'expert'}, dimensions={1} | all-to-all | bytes 3145728 | tf_op jit(solution)/shard_map/all_to_all | solution.py:105
  180.3 34.5 %reduce-scatter.11.cloned.1.call-done = f32[2,512,192]{1,2,0:T(8,128)} async-done(((f32[2,512,768]{1,2,0:T(8,128)}), f32[2,512,192]{1,2,0:T(8,128)}) %reduce-scatter.11.cloned.1.call-update) | async-done | bytes 786448 | tf_op jit(solution)/shard_map/reduce_scatter | solution.py:109
  224.2 11.7 all-to-all-done.1
  241.9 11.7 all_gather.92
  282.2 55.6 %all-gather.63.cloned.1.call-done = f32[4,394,768]{2,1,0:T(8,128)} async-done(((f32[1,394,768]{2,1,0:T(8,128)}), f32[4,394,768]{2,1,0:T(8,128)}) %all-gather.63.cloned.1.call-update) | async-done | bytes 4841488 | tf_op jit(solution)/shard_map/all_gather | solution.py:17
  351.3 41.3 %all_to_all.101 = bf16[2,512,768]{2,0,1:T(2,128)(2,1)} all-to-all(bf16[2,512,768]{2,0,1:T(2,128)(2,1)S(1)} %copy.1240), channel_id=1, replica_groups=mesh['section'=2,'expert'=4,'tensor'=4] {'expert'}, dimensions={1} | all-to-all | bytes 3145728 | tf_op jit(solution)/shard_map/all_to_all | solution.py:105
  407.5 42.2 %reduce-scatter.13.cloned.1.call-done = f32[2,512,192]{1,2,0:T(8,128)} async-done(((f32[2,512,768]{1,2,0:T(8,128)}), f32[2,512,192]{1,2,0:T(8,128)}) %reduce-scatter.13.cloned.1.call-update) | async-done | bytes 786448 | tf_op jit(solution)/shard_map/reduce_scatter | solution.py:109
  459.3 11.6 all-to-all-done.3
  476.8 11.7 all_gather.95
  521.0 55.5 %all-gather.65.cloned.1.call-done = f32[4,394,768]{2,1,0:T(8,128)} async-done(((f32[1,394,768]{2,1,0:T(8,128)}), f32[4,394,768]{2,1,0:T(8,128)}) %all-gather.65.cloned.1.call-update) | async-done | bytes 4841488 | tf_op jit(solution)/shard_map/all_gather | solution.py:17
  587.3 41.7 %all_to_all.102 = bf16[2,512,768]{2,0,1:T(2,128)(2,1)} all-to-all(bf16[2,512,768]{2,0,1:T(2,128)(2,1)S(1)} %copy.1258), channel_id=1, replica_groups=mesh['section'=2,'expert'=4,'tensor'=4] {'expert'}, dimensions={1} | all-to-all | bytes 3145728 | tf_op jit(solution)/shard_map/all_to_all | solution.py:105
  644.0 42.2 %reduce-scatter.15.cloned.1.call-done = f32[2,512,192]{1,2,0:T(8,128)} async-done(((f32[2,512,768]{1,2,0:T(8,128)}), f32[2,512,192]{1,2,0:T(8,128)}) %reduce-scatter.15.cloned.1.call-update) | async-done | bytes 786448 | tf_op jit(solution)/shard_map/reduce_scatter | solution.py:109
  694.4 13.0 all-to-all-done.5
  710.4 11.8 all_gather.98
  736.4 55.8 %all-gather.67.cloned.1.call-done = f32[4,394,768]{2,1,0:T(8,128)} async-done(((f32[1,394,768]{2,1,0:T(8,128)}), f32[4,394,768]{2,1,0:T(8,128)}) %all-gather.67.cloned.1.call-update) | async-done | bytes 4841488 | tf_op jit(solution)/shard_map/all_gather | solution.py:17
  803.1 41.3 %all_to_all.103 = bf16[2,512,768]{2,0,1:T(2,128)(2,1)} all-to-all(bf16[2,512,768]{2,0,1:T(2,128)(2,1)S(1)} %copy.1276), channel_id=1, replica_groups=mesh['section'=2,'expert'=4,'tensor'=4] {'expert'}, dimensions={1} | all-to-all | bytes 3145728 | tf_op jit(solution)/shard_map/all_to_all | solution.py:105
  859.3 42.2 %reduce-scatter.17.cloned.1.call-done = f32[2,512,192]{1,2,0:T(8,128)} async-done(((f32[2,512,768]{1,2,0:T(8,128)}), f32[2,512,192]{1,2,0:T(8,128)}) %reduce-scatter.17.cloned.1.call-update) | async-done | bytes 786448 | tf_op jit(solution)/shard_map/reduce_scatter | solution.py:109
  909.7 13.0 all-to-all-done.7
  925.7 11.7 all_gather.101
  948.5 55.9 %all-gather.69.cloned.1.call-done = f32[4,394,768]{2,1,0:T(8,128)} async-done(((f32[1,394,768]{2,1,0:T(8,128)}), f32[4,394,768]{2,1,0:T(8,128)}) %all-gather.69.cloned.1.call-update) | async-done | bytes 4841488 | tf_op jit(solution)/shard_map/all_gather | solution.py:17
  1015.3 41.3 %all_to_all.104 = bf16[2,512,768]{2,0,1:T(2,128)(2,1)} all-to-all(bf16[2,512,768]{2,0,1:T(2,128)(2,1)S(1)} %copy.1292), channel_id=1, replica_groups=mesh['section'=2,'expert'=4,'tensor'=4] {'expert'}, dimensions={1} | all-to-all | bytes 3145728 | tf_op jit(solution)/shard_map/all_to_all | solution.py:105
  1070.0 42.1 %reduce-scatter.19.cloned.1.call-done = f32[2,512,192]{1,2,0:T(8,128)} async-done(((f32[2,512,768]{1,2,0:T(8,128)}), f32[2,512,192]{1,2,0:T(8,128)}) %reduce-scatter.19.cloned.1.call-update) | async-done | bytes 786448 | tf_op jit(solution)/shard_map/reduce_scatter | solution.py:109
  1113.8 19.1 all_to_all.105
  1137.8 8.9 gather_fusion
  1166.8 13.0 all-gather.35.cloned.1.call-done
  1184.9 18.7 all_to_all.106
  1204.8 29.1 %all-gather.31.cloned.1.call-done = bf16[2,512,768]{1,2,0:T(8,128)(2,1)} async-done(((bf16[2,512,192]{1,2,0:T(8,128)(2,1)}), bf16[2,512,768]{1,2,0:T(8,128)(2,1)}) %all-gather.31.cloned.1.call-update) | async-done | bytes 1572880 | tf_op jit(solution)/shard_map/all_gather | solution.py:182
  1243.7 44.0 %reduce-scatter.21.cloned.1.call-done = f32[2,512,192]{1,2,0:T(8,128)} async-done(((f32[2,512,768]{1,2,0:T(8,128)}), f32[2,512,192]{1,2,0:T(8,128)}) %reduce-scatter.21.cloned.1.call-update) | async-done | bytes 786448 | tf_op jit(solution)/shard_map/reduce_scatter | solution.py:194
  1289.4 18.7 all_to_all.107
  1312.5 26.4 all-gather.33.cloned.1.call-done
  1359.5 60.8 %all-reduce.9.cloned.1.call-done = f32[394,768]{0,1:T(8,128)} async-done(((f32[394,768]{0,1:T(8,128)}), f32[394,768]{0,1:T(8,128)}) %all-reduce.9.cloned.1.call-update) | async-done | bytes 1210384 | tf_op jit(solution)/shard_map/psum | solution.py:254
  1435.6 19.2 all_to_all.108
  1456.3 28.7 %all-gather.37.cloned.1.call-done = bf16[2,512,768]{1,2,0:T(8,128)(2,1)} async-done(((bf16[2,512,192]{1,2,0:T(8,128)(2,1)}), bf16[2,512,768]{1,2,0:T(8,128)(2,1)}) %all-gather.37.cloned.1.call-update) | async-done | bytes 1572880 | tf_op jit(solution)/shard_map/all_gather | solution.py:182
  1495.4 43.4 %reduce-scatter.23.cloned.1.call-done = f32[2,512,192]{1,2,0:T(8,128)} async-done(((f32[2,512,768]{1,2,0:T(8,128)}), f32[2,512,192]{1,2,0:T(8,128)}) %reduce-scatter.23.cloned.1.call-update) | async-done | bytes 786448 | tf_op jit(solution)/shard_map/reduce_scatter | solution.py:194
  1540.5 18.7 all_to_all.109
  1561.1 23.3 all-gather.41.cloned.1.call-done
  1590.6 27.2 %all-gather.39.cloned.1.call-done = bf16[2,512,768]{1,0,2:T(2,128)(2,1)} async-done(((bf16[2,512,192]{1,0,2:T(2,128)(2,1)}), bf16[2,512,768]{1,0,2:T(2,128)(2,1)}) %all-gather.39.cloned.1.call-update) | async-done | bytes 1572880 | tf_op jit(solution)/shard_map/all_gather | solution.py:198
  1644.0 52.6 %all-reduce.11.cloned.1.call-done = f32[394,768]{0,1:T(8,128)} async-done(((f32[394,768]{0,1:T(8,128)}), f32[394,768]{0,1:T(8,128)}) %all-reduce.11.cloned.1.call-update) | async-done | bytes 1210384 | tf_op jit(solution)/shard_map/psum | solution.py:254
  1712.4 19.2 all_to_all.110
  1732.7 29.1 %all-gather.43.cloned.1.call-done = bf16[2,512,768]{1,2,0:T(8,128)(2,1)} async-done(((bf16[2,512,192]{1,2,0:T(8,128)(2,1)}), bf16[2,512,768]{1,2,0:T(8,128)(2,1)}) %all-gather.43.cloned.1.call-update) | async-done | bytes 1572880 | tf_op jit(solution)/shard_map/all_gather | solution.py:182
  1772.4 43.3 %reduce-scatter.25.cloned.1.call-done = f32[2,512,192]{1,2,0:T(8,128)} async-done(((f32[2,512,768]{1,2,0:T(8,128)}), f32[2,512,192]{1,2,0:T(8,128)}) %reduce-scatter.25.cloned.1.call-update) | async-done | bytes 786448 | tf_op jit(solution)/shard_map/reduce_scatter | solution.py:194
  1817.3 18.7 all_to_all.111
  1838.1 23.3 all-gather.47.cloned.1.call-done
  1866.9 27.6 %all-gather.45.cloned.1.call-done = bf16[2,512,768]{1,0,2:T(2,128)(2,1)} async-done(((bf16[2,512,192]{1,0,2:T(2,128)(2,1)}), bf16[2,512,768]{1,0,2:T(2,128)(2,1)}) %all-gather.45.cloned.1.call-update) | async-done | bytes 1572880 | tf_op jit(solution)/shard_map/all_gather | solution.py:198
  1920.6 52.5 %all-reduce.13.cloned.1.call-done = f32[394,768]{0,1:T(8,128)} async-done(((f32[394,768]{0,1:T(8,128)}), f32[394,768]{0,1:T(8,128)}) %all-reduce.13.cloned.1.call-update) | async-done | bytes 1210384 | tf_op jit(solution)/shard_map/psum | solution.py:254
  1988.8 19.2 all_to_all.112
  2009.5 28.7 %all-gather.49.cloned.1.call-done = bf16[2,512,768]{1,2,0:T(8,128)(2,1)} async-done(((bf16[2,512,192]{1,2,0:T(8,128)(2,1)}), bf16[2,512,768]{1,2,0:T(8,128)(2,1)}) %all-gather.49.cloned.1.call-update) | async-done | bytes 1572880 | tf_op jit(solution)/shard_map/all_gather | solution.py:182
  2048.8 43.3 %reduce-scatter.27.cloned.1.call-done = f32[2,512,192]{1,2,0:T(8,128)} async-done(((f32[2,512,768]{1,2,0:T(8,128)}), f32[2,512,192]{1,2,0:T(8,128)}) %reduce-scatter.27.cloned.1.call-update) | async-done | bytes 786448 | tf_op jit(solution)/shard_map/reduce_scatter | solution.py:194
  2093.7 18.7 all_to_all.113
  2114.3 23.5 all-gather.53.cloned.1.call-done
  2143.3 27.7 %all-gather.51.cloned.1.call-done = bf16[2,512,768]{1,0,2:T(2,128)(2,1)} async-done(((bf16[2,512,192]{1,0,2:T(2,128)(2,1)}), bf16[2,512,768]{1,0,2:T(2,128)(2,1)}) %all-gather.51.cloned.1.call-update) | async-done | bytes 1572880 | tf_op jit(solution)/shard_map/all_gather | solution.py:198
  2202.7 49.9 %all-reduce.15.cloned.1.call-done = f32[394,768]{0,1:T(8,128)} async-done(((f32[394,768]{0,1:T(8,128)}), f32[394,768]{0,1:T(8,128)}) %all-reduce.15.cloned.1.call-update) | async-done | bytes 1210384 | tf_op jit(solution)/shard_map/psum | solution.py:254
  2275.1 19.1 all_to_all.114
  2296.2 29.1 %all-gather.55.cloned.1.call-done = bf16[2,512,768]{1,2,0:T(8,128)(2,1)} async-done(((bf16[2,512,192]{1,2,0:T(8,128)(2,1)}), bf16[2,512,768]{1,2,0:T(8,128)(2,1)}) %all-gather.55.cloned.1.call-update) | async-done | bytes 1572880 | tf_op jit(solution)/shard_map/all_gather | solution.py:182
  2381.9 15.9 all_gather.104
  2408.6 6.5 scatter_fusion
  2494.2 7.3 add_bitcast_fusion
  2501.6 13.9 all-gather.57.cloned.1.call-done
  2546.6 10.2 add_bitcast_fusion.1
  2556.9 41.4 %all-reduce.17.cloned.1.call-done = f32[394,768]{0,1:T(8,128)} async-done(((f32[394,768]{0,1:T(8,128)}), f32[394,768]{0,1:T(8,128)}) %all-reduce.17.cloned.1.call-update) | async-done | bytes 1210384 | tf_op jit(solution)/shard_map/psum | solution.py:254
  2614.6 8.7 scatter_fusion.1
  2629.7 21.7 all-reduce
  2651.4 45.9 %all-reduce.19.cloned.1.call-done = (f32[1,3,768,192]{2,3,1,0:T(8,128)}, f32[1,192,768]{2,1,0:T(8,128)}) async-done(((f32[1,3,768,192]{2,3,1,0:T(8,128)}, f32[1,192,768]{2,1,0:T(8,128)}), (f32[1,3,768,192]{2,3,1,0:T(8,128)}, f32[1,192,768]{2,1,0:T(8,128)})) %all-reduce.19.cloned.1.call-update) | async-done | bytes 2359312 | tf_op jit(solution)/shard_map/psum | solution.py:367
  (1413 shorter events, 810.9 us)
Async XLA Ops:
  7.2 89.5 %all-gather.61.cloned.1.call-start = ((), (), s32[]{:S(2)}) async-start(), calls=%async_computation.60 | async-start | bytes 6144000 | tf_op jit(solution)/shard_map/all_gather | solution.py:17
  35.2 179.6 %reduce-scatter.11.cloned.1.call-start = ((), (), s32[]{:S(2)}) async-start(), calls=%async_computation.30 | async-start | bytes 3932160 | tf_op jit(solution)/shard_map/reduce_scatter | solution.py:109
  43.5 195.5 %copy-start.317 = (s32[394,2]{0,1:T(2,128)}, s32[394,2]{0,1:T(2,128)S(1)}, u32[]{:S(2)}) copy-start(s32[394,2]{0,1:T(2,128)S(1)} %compare_select_fusion.4) | copy-start | bytes 9460
  217.1 18.9 all-to-all-start.1
  221.7 116.2 %all-gather.63.cloned.1.call-start = ((), (), s32[]{:S(2)}) async-start(), calls=%async_computation.61 | async-start | bytes 6144000 | tf_op jit(solution)/shard_map/all_gather | solution.py:17
  255.8 15.9 collective-permute-start
  280.4 169.3 %reduce-scatter.13.cloned.1.call-start = ((), (), s32[]{:S(2)}) async-start(), calls=%async_computation.31 | async-start | bytes 3932160 | tf_op jit(solution)/shard_map/reduce_scatter | solution.py:109
  280.9 192.9 %copy-start.319 = (s32[394,2]{0,1:T(2,128)}, s32[394,2]{0,1:T(2,128)S(1)}, u32[]{:S(2)}) copy-start(s32[394,2]{0,1:T(2,128)S(1)} %compare_select_fusion.3) | copy-start | bytes 9460
  346.6 109.9 %copy-start.217 = (f32[394]{0:T(512)}, f32[394]{0:T(512)S(1)}, u32[]{:S(2)}) copy-start(f32[394]{0:T(512)S(1)} %broadcast_multiply_fusion.28) | copy-start | bytes 4732
  451.9 18.9 all-to-all-start.3
  456.5 120.0 %all-gather.65.cloned.1.call-start = ((), (), s32[]{:S(2)}) async-start(), calls=%async_computation.62 | async-start | bytes 6144000 | tf_op jit(solution)/shard_map/all_gather | solution.py:17
  490.6 19.6 collective-permute-start.1
  519.0 167.2 %reduce-scatter.15.cloned.1.call-start = ((), (), s32[]{:S(2)}) async-start(), calls=%async_computation.32 | async-start | bytes 3932160 | tf_op jit(solution)/shard_map/reduce_scatter | solution.py:109
  519.7 188.8 %copy-start.325 = (s32[394,2]{0,1:T(2,128)}, s32[394,2]{0,1:T(2,128)S(1)}, u32[]{:S(2)}) copy-start(s32[394,2]{0,1:T(2,128)S(1)} %get-tuple-element.255) | copy-start | bytes 9460
  582.7 127.6 %copy-start.6 = (f32[394,768]{0,1:T(8,128)}, f32[394,768]{0,1:T(8,128)S(1)}, u32[]{:S(2)}) copy-start(f32[394,768]{0,1:T(8,128)S(1)} %get-tuple-element.147) | copy-start | bytes 3631108
  582.7 110.4 %copy-start.220 = (f32[394]{0:T(512)}, f32[394]{0:T(512)S(1)}, u32[]{:S(2)}) copy-start(f32[394]{0:T(512)S(1)} %broadcast_multiply_fusion.26) | copy-start | bytes 4732
  688.5 18.9 all-to-all-start.5
  693.1 99.2 %all-gather.67.cloned.1.call-start = ((), (), s32[]{:S(2)}) async-start(), calls=%async_computation.63 | async-start | bytes 6144000 | tf_op jit(solution)/shard_map/all_gather | solution.py:17
  723.3 4.1 collective-permute-start.2
  734.9 166.5 %reduce-scatter.17.cloned.1.call-start = ((), (), s32[]{:S(2)}) async-start(), calls=%async_computation.33 | async-start | bytes 3932160 | tf_op jit(solution)/shard_map/reduce_scatter | solution.py:109
  798.4 127.2 %copy-start.9 = (f32[394,768]{0,1:T(8,128)}, f32[394,768]{0,1:T(8,128)S(1)}, u32[]{:S(2)}) copy-start(f32[394,768]{0,1:T(8,128)S(1)} %get-tuple-element.141) | copy-start | bytes 3631108
  903.8 18.9 all-to-all-start.7
  908.4 96.1 %all-gather.69.cloned.1.call-start = ((), (), s32[]{:S(2)}) async-start(), calls=%async_computation.64 | async-start | bytes 6144000 | tf_op jit(solution)/shard_map/all_gather | solution.py:17
  909.7 677.2 %copy-start.184 = (f32[394,8]{0,1:T(8,128)}, f32[394,8]{0,1:T(8,128)S(1)}, u32[]{:S(2)}) copy-start(f32[394,8]{0,1:T(8,128)S(1)} %fusion.416) | copy-start | bytes 37828
  938.5 3.1 collective-permute-start.3
  947.2 165.0 %reduce-scatter.19.cloned.1.call-start = ((), (), s32[]{:S(2)}) async-start(), calls=%async_computation.34 | async-start | bytes 3932160 | tf_op jit(solution)/shard_map/reduce_scatter | solution.py:109
  1010.7 337.5 %copy-start.226 = (f32[394]{0:T(512)}, f32[394]{0:T(512)S(1)}, u32[]{:S(2)}) copy-start(f32[394]{0:T(512)S(1)} %broadcast_multiply_fusion.22) | copy-start | bytes 4732
  1012.4 335.8 %copy-start.263 = (f32[394]{0:T(512)}, f32[394]{0:T(512)S(1)}, u32[]{:S(2)}) copy-start(f32[394]{0:T(512)S(1)} %add_rsqrt_fusion.2) | copy-start | bytes 4732
  1070.0 109.9 %all-gather.35.cloned.1.call-start = ((), (), s32[]{:S(2)}) async-start(), calls=%async_computation.38 | async-start | bytes 3932160 | tf_op jit(solution)/shard_map/all_gather | solution.py:121
  1137.7 96.2 %all-gather.31.cloned.1.call-start = ((), (), s32[]{:S(2)}) async-start(), calls=%async_computation.35 | async-start | bytes 1966080 | tf_op jit(solution)/shard_map/all_gather | solution.py:182
  1166.8 143.2 %copy-start.192 = (f32[394,8]{0,1:T(8,128)}, f32[394,8]{0,1:T(8,128)S(1)}, u32[]{:S(2)}) copy-start(f32[394,8]{0,1:T(8,128)S(1)} %fusion.418) | copy-start | bytes 37828
  1182.8 127.2 %copy-start.194 = (f32[394,8]{0,1:T(8,128)}, f32[394,8]{0,1:T(8,128)S(1)}, u32[]{:S(2)}) copy-start(f32[394,8]{0,1:T(8,128)S(1)} %get-tuple-element.129) | copy-start | bytes 37828
  1204.7 83.0 %reduce-scatter.21.cloned.1.call-start = ((), (), s32[]{:S(2)}) async-start(), calls=%async_computation.36 | async-start | bytes 3932160 | tf_op jit(solution)/shard_map/reduce_scatter | solution.py:194
  1243.6 95.3 %all-gather.33.cloned.1.call-start = ((), (), s32[]{:S(2)}) async-start(), calls=%async_computation.37 | async-start | bytes 1966080 | tf_op jit(solution)/shard_map/all_gather | solution.py:198
  1309.8 110.5 %all-reduce.9.cloned.1.call-start = ((), (), s32[]{:S(2)}) async-start(), calls=%async_computation.39 | async-start | bytes 3145728 | tf_op jit(solution)/shard_map/psum | solution.py:254
  1359.4 125.6 %all-gather.37.cloned.1.call-start = ((), (), s32[]{:S(2)}) async-start(), calls=%async_computation.40 | async-start | bytes 1966080 | tf_op jit(solution)/shard_map/all_gather | solution.py:182
  1427.9 3.9 collective-permute-start.4
  1433.4 151.1 %copy-start.70 = (f32[394,768]{0,1:T(8,128)}, f32[394,768]{0,1:T(8,128)S(1)}, u32[]{:S(2)}) copy-start(f32[394,768]{0,1:T(8,128)S(1)} %fusion.267) | copy-start | bytes 3631108
  1455.9 83.0 %reduce-scatter.23.cloned.1.call-start = ((), (), s32[]{:S(2)}) async-start(), calls=%async_computation.41 | async-start | bytes 3932160 | tf_op jit(solution)/shard_map/reduce_scatter | solution.py:194
  1494.8 89.6 %all-gather.41.cloned.1.call-start = ((), (), s32[]{:S(2)}) async-start(), calls=%async_computation.43 | async-start | bytes 3932160 | tf_op jit(solution)/shard_map/all_gather | solution.py:121
  1495.4 122.3 %all-gather.39.cloned.1.call-start = ((), (), s32[]{:S(2)}) async-start(), calls=%async_computation.42 | async-start | bytes 1966080 | tf_op jit(solution)/shard_map/all_gather | solution.py:198
  1561.0 135.7 %all-reduce.11.cloned.1.call-start = ((), (), s32[]{:S(2)}) async-start(), calls=%async_computation.44 | async-start | bytes 3145728 | tf_op jit(solution)/shard_map/psum | solution.py:254
  1635.8 126.0 %all-gather.43.cloned.1.call-start = ((), (), s32[]{:S(2)}) async-start(), calls=%async_computation.45 | async-start | bytes 1966080 | tf_op jit(solution)/shard_map/all_gather | solution.py:182
  1704.7 3.9 collective-permute-start.5
  1710.2 151.2 %copy-start.72 = (f32[394,768]{0,1:T(8,128)}, f32[394,768]{0,1:T(8,128)S(1)}, u32[]{:S(2)}) copy-start(f32[394,768]{0,1:T(8,128)S(1)} %fusion.266) | copy-start | bytes 3631108
  1732.7 83.0 %reduce-scatter.25.cloned.1.call-start = ((), (), s32[]{:S(2)}) async-start(), calls=%async_computation.46 | async-start | bytes 3932160 | tf_op jit(solution)/shard_map/reduce_scatter | solution.py:194
  1771.6 89.8 %all-gather.47.cloned.1.call-start = ((), (), s32[]{:S(2)}) async-start(), calls=%async_computation.48 | async-start | bytes 3932160 | tf_op jit(solution)/shard_map/all_gather | solution.py:121
  1772.3 122.2 %all-gather.45.cloned.1.call-start = ((), (), s32[]{:S(2)}) async-start(), calls=%async_computation.47 | async-start | bytes 1966080 | tf_op jit(solution)/shard_map/all_gather | solution.py:198
  1837.8 135.3 %all-reduce.13.cloned.1.call-start = ((), (), s32[]{:S(2)}) async-start(), calls=%async_computation.49 | async-start | bytes 3145728 | tf_op jit(solution)/shard_map/psum | solution.py:254
  1912.2 126.0 %all-gather.49.cloned.1.call-start = ((), (), s32[]{:S(2)}) async-start(), calls=%async_computation.50 | async-start | bytes 1966080 | tf_op jit(solution)/shard_map/all_gather | solution.py:182
  1981.1 3.9 collective-permute-start.6
  1986.6 151.2 %copy-start.74 = (f32[394,768]{0,1:T(8,128)}, f32[394,768]{0,1:T(8,128)S(1)}, u32[]{:S(2)}) copy-start(f32[394,768]{0,1:T(8,128)S(1)} %fusion.265) | copy-start | bytes 3631108
  2009.1 83.0 %reduce-scatter.27.cloned.1.call-start = ((), (), s32[]{:S(2)}) async-start(), calls=%async_computation.51 | async-start | bytes 3932160 | tf_op jit(solution)/shard_map/reduce_scatter | solution.py:194
  2048.0 89.8 %all-gather.53.cloned.1.call-start = ((), (), s32[]{:S(2)}) async-start(), calls=%async_computation.53 | async-start | bytes 3932160 | tf_op jit(solution)/shard_map/all_gather | solution.py:121
  2048.7 122.3 %all-gather.51.cloned.1.call-start = ((), (), s32[]{:S(2)}) async-start(), calls=%async_computation.52 | async-start | bytes 1966080 | tf_op jit(solution)/shard_map/all_gather | solution.py:198
  2114.1 138.5 %all-reduce.15.cloned.1.call-start = ((), (), s32[]{:S(2)}) async-start(), calls=%async_computation.54 | async-start | bytes 3145728 | tf_op jit(solution)/shard_map/psum | solution.py:254
  2191.7 133.5 %all-gather.55.cloned.1.call-start = ((), (), s32[]{:S(2)}) async-start(), calls=%async_computation.55 | async-start | bytes 1966080 | tf_op jit(solution)/shard_map/all_gather | solution.py:182
  2261.6 4.3 collective-permute-start.7
  2296.2 163.6 %reduce-scatter.29.cloned.1.call-start = ((), (), s32[]{:S(2)}) async-start(), calls=%async_computation.56 | async-start | bytes 3932160 | tf_op jit(solution)/shard_map/reduce_scatter | solution.py:194
  2335.1 149.0 %all-gather.59.cloned.1.call-start = ((), (), s32[]{:S(2)}) async-start(), calls=%async_computation.58 | async-start | bytes 3932160 | tf_op jit(solution)/shard_map/all_gather | solution.py:121
  2462.0 20.2 all-to-all-start.19
  2466.6 48.9 %all-gather.57.cloned.1.call-start = ((), (), s32[]{:S(2)}) async-start(), calls=%async_computation.57 | async-start | bytes 1966080 | tf_op jit(solution)/shard_map/all_gather | solution.py:198
  2484.0 114.2 %all-reduce.17.cloned.1.call-start = ((), (), s32[]{:S(2)}) async-start(), calls=%async_computation.59 | async-start | bytes 3145728 | tf_op jit(solution)/shard_map/psum | solution.py:254
  2537.4 159.9 %all-reduce.19.cloned.1.call-start = ((), (), s32[]{:S(2)}) async-start(), calls=%async_computation.65 | async-start | bytes 4718592 | tf_op jit(solution)/shard_map/psum | solution.py:367
  (362 other events, 3947.5 us)
Sparse Core Ops, SparseCore 0:
  35.3 61.2 all-gather.60
  172.7 42.0 reduce-scatter.10
  280.5 57.2 all-gather.62
  407.6 42.0 reduce-scatter.12
  519.1 57.3 all-gather.64
  644.1 42.0 reduce-scatter.14
  735.1 57.1 all-gather.66
  859.4 42.0 reduce-scatter.16
  947.3 57.1 all-gather.68
  1070.1 42.0 reduce-scatter.18
  1137.8 41.9 all-gather.34
  1204.9 28.9 all-gather.30
  1243.8 43.8 reduce-scatter.20
  1309.9 28.9 all-gather.32
  1359.5 60.7 all-reduce.8
  1456.0 28.9 all-gather.36
  1494.9 43.8 reduce-scatter.22
  1540.5 43.8 all-gather.40
  1586.8 30.8 all-gather.38
  1635.9 60.7 all-reduce.10
  1732.8 28.9 all-gather.42
  1771.7 43.8 reduce-scatter.24
  1817.5 43.8 all-gather.46
  1863.6 30.8 all-gather.44
  1912.3 60.7 all-reduce.12
  2009.2 28.9 all-gather.48
  2048.1 43.8 reduce-scatter.26
  2093.9 43.8 all-gather.52
  2140.1 30.8 all-gather.50
  2191.8 60.7 all-reduce.14
  2296.3 28.9 all-gather.54
  2335.2 43.8 reduce-scatter.28
  2380.8 45.9 all-gather.58
  2484.0 31.3 all-gather.56
  2537.5 60.7 all-reduce.16
  2601.1 96.1 all-reduce.18
